TPU v7x, 256 devices: a whole 4x4x8 slice. The times are simulated.
256 devices in a mesh: tm: 8 (over z), height: 16 (over x, y), cam: 2 (over core).
Axes of the slice: x: 4, y: 4, z: 8, core: 2. Of those that a mesh axis runs over, the one named last changes fastest.
Arguments:
- video_clip: bfloat16 [2, 32, 128, 64, 256], P('cam', 'tm', 'height'), may hold values from -6 to 6
- valid_from: int32 [2], P('cam'), may hold values from 0 to 16, as said below
- norm_gain: float32 [256], replicated, may hold values from 0.5 to 1.5
- spatial_weight: bfloat16 [3, 3, 256, 256], replicated, may hold values from -0.125 to 0.125
- temporal_weight: bfloat16 [3, 256, 256], replicated, may hold values from -0.21875 to 0.21875
- mix_weight: bfloat16 [3, 256, 256], replicated, may hold values from -0.21875 to 0.21875
- cotangent: bfloat16 [2, 16, 128, 64, 256], P('cam', None, ('height', 'tm')), may hold values from -6 to 6
Outputs:
- encoded: bfloat16 [2, 16, 128, 64, 256], P('cam', None, ('height', 'tm'))
- video_gradient: bfloat16 [2, 32, 128, 64, 256], P('cam', 'tm', 'height')
- spatial_gradient: float32 [3, 3, 256, 256], replicated
- temporal_gradient: float32 [3, 256, 256], replicated
- mix_gradient: float32 [3, 256, 256], replicated
- gain_gradient: float32 [256], replicated
Inputs may be any that keep to these rules, and one draw needn't show every extreme that they name: Frames before valid_from of a camera are padding. In every draw some camera starts at 16.
All inputs are finite; a program needn't handle non-finite values.
Results may differ from a plain program's by a relative error of at most 0.0065.
Values may be sent and summed in bfloat16 or wider, within the bound.
A program may use at most 128 MiB of HBM per device.

v0:
```python
import math
import jax
import jax.numpy as jnp
from jax import lax
from jax.sharding import PartitionSpec as P


def extended(array, sides, width):
    for axis, dim in sides:
        size, length = (lax.axis_size(axis), array.shape[dim])
        up = [(i, (i + 1) % size) for i in range(size - 1)]
        down = [(j, i) for i, j in up]
        last = lax.slice_in_dim(array, length - width, length, axis=dim)
        initial = lax.slice_in_dim(array, 0, width, axis=dim)
        before = lax.ppermute(last, axis, up)
        after = lax.ppermute(initial, axis, down)
        array = jnp.concatenate([before, array, after], axis=dim)
    return array


def shifted(block, axis, distance):
    devices = range(lax.axis_size(axis))
    route = [(i - distance, i) for i in devices if i - distance in devices]
    return lax.ppermute(block, axis, route)


def project(rows_in, weight):
    flat_rows = rows_in.reshape(-1, rows_in.shape[-1])
    product = jnp.dot(flat_rows, weight, preferred_element_type=jnp.float32)
    return product.reshape(rows_in.shape[:-1] + (weight.shape[-1],))


def project_back(rows_in, weight):
    flat_rows = rows_in.reshape(-1, rows_in.shape[-1])
    product = lax.dot_general(
        flat_rows, weight, (((1,), (1,)), ((), ())), preferred_element_type=jnp.float32
    )
    return product.reshape(rows_in.shape[:-1] + (weight.shape[0],))


def outer_sum(left_rows, right_rows):
    return lax.dot_general(
        left_rows.reshape(-1, left_rows.shape[-1]),
        right_rows.reshape(-1, right_rows.shape[-1]),
        (((0,), (0,)), ((), ())),
        preferred_element_type=jnp.float32,
    )


def column_pad(padded):
    return jnp.pad(padded, ((0, 0), (0, 0), (0, 0), (1, 1), (0, 0)))


def spatial(padded, weight):
    columns = column_pad(padded)
    rows_here = padded.shape[2] - 2
    width_here = padded.shape[3]
    accumulated = jnp.zeros(
        padded.shape[:2] + (rows_here, width_here, weight.shape[-1]), jnp.float32
    )
    for row_tap in range(3):
        for column_tap in range(3):
            window = columns[
                :, :, row_tap : row_tap + rows_here, column_tap : column_tap + width_here
            ]
            accumulated = accumulated + project(window, weight[row_tap, column_tap])
    return accumulated


def spatial_grad(padded, gradient):
    columns = column_pad(padded)
    rows_here = padded.shape[2] - 2
    width_here = padded.shape[3]
    outer_rows = []
    for row_tap in range(3):
        inner_rows = []
        for column_tap in range(3):
            window = columns[
                :, :, row_tap : row_tap + rows_here, column_tap : column_tap + width_here
            ]
            inner_rows.append(outer_sum(window, gradient))
        outer_rows.append(jnp.stack(inner_rows))
    return jnp.stack(outer_rows)


def flipped(weight):
    return jnp.transpose(weight[::-1, ::-1], (0, 1, 3, 2))


def norm_forward(masked, norm_gain):
    values = masked.astype(jnp.float32)
    inverse = lax.rsqrt(jnp.mean(values * values, axis=-1, keepdims=True) + 1e-06)
    unit_rows = values * inverse
    return ((unit_rows * norm_gain).astype(jnp.bfloat16), unit_rows, inverse)


def norm_backward(normed_gradient, unit_rows, inverse, norm_gain, present):
    unit_gradient = normed_gradient * norm_gain
    masked_gradient = inverse * (
        unit_gradient - unit_rows * jnp.mean(unit_gradient * unit_rows, axis=-1, keepdims=True)
    )
    video_gradient = jnp.where(present, masked_gradient, jnp.zeros_like(masked_gradient)).astype(
        jnp.bfloat16
    )
    gain_gradient = jnp.sum((normed_gradient * unit_rows).reshape(-1, unit_rows.shape[-1]), axis=0)
    return (video_gradient, gain_gradient)


def split_frames(active, prior_frame):
    dims_in = active.shape
    frame_pairs = active.reshape(dims_in[0], dims_in[1] // 2, 2, dims_in[2], dims_in[3], dims_in[4])
    even_frames = frame_pairs[:, :, 0]
    odd_frames = frame_pairs[:, :, 1]
    prior_odd = jnp.concatenate([prior_frame, odd_frames[:, :-1]], axis=1)
    return (even_frames, odd_frames, prior_odd)


def temporal_forward(even_frames, odd_frames, prior_odd, weight):
    accumulated = (
        project(odd_frames, weight[0])
        + project(even_frames, weight[1])
        + project(prior_odd, weight[2])
    )
    return accumulated.astype(jnp.bfloat16)


def temporal_backward(even_frames, odd_frames, prior_odd, strided_gradient, following, weight):
    weight_gradient = jnp.stack(
        [
            outer_sum(odd_frames, strided_gradient),
            outer_sum(even_frames, strided_gradient),
            outer_sum(prior_odd, strided_gradient),
        ]
    )
    next_gradient = jnp.concatenate([strided_gradient[:, 1:], following], axis=1)
    odd_gradient = project_back(strided_gradient, weight[0]) + project_back(
        next_gradient, weight[2]
    )
    even_gradient = project_back(strided_gradient, weight[1])
    dims_in = even_frames.shape
    active_gradient = jnp.stack([even_gradient, odd_gradient], axis=2).reshape(
        dims_in[0], dims_in[1] * 2, dims_in[2], dims_in[3], dims_in[4]
    )
    return (active_gradient, weight_gradient)


def mix_forward(regrouped, weight):
    frame_count = regrouped.shape[1]
    blank_frames = jnp.zeros(regrouped.shape[:1] + (2,) + regrouped.shape[2:], regrouped.dtype)
    history = jnp.concatenate([blank_frames, regrouped], axis=1)
    accumulated = regrouped.astype(jnp.float32)
    for offset in range(3):
        accumulated = accumulated + project(
            history[:, 2 - offset : 2 - offset + frame_count], weight[offset]
        )
    return (accumulated.astype(jnp.bfloat16), history)


def mix_backward(history, cotangent, weight):
    frame_count = cotangent.shape[1]
    mix_gradient = jnp.stack(
        [
            outer_sum(history[:, 2 - offset : 2 - offset + frame_count], cotangent)
            for offset in range(3)
        ]
    )
    blank_frames = jnp.zeros(cotangent.shape[:1] + (2,) + cotangent.shape[2:], cotangent.dtype)
    ahead = jnp.concatenate([cotangent, blank_frames], axis=1)
    accumulated = cotangent.astype(jnp.float32)
    for offset in range(3):
        accumulated = accumulated + project_back(
            ahead[:, offset : offset + frame_count], weight[offset]
        )
    return (mix_gradient, accumulated.astype(jnp.bfloat16))


def activation_backward(active_gradient, pre_activation):
    sigmoid_value = jax.nn.sigmoid(pre_activation)
    return (
        active_gradient * sigmoid_value * (1.0 + pre_activation * (1.0 - sigmoid_value))
    ).astype(jnp.bfloat16)


def on_device(
    video_clip, valid_from, norm_gain, spatial_weight, temporal_weight, mix_weight, cotangent
):
    frames_here = video_clip.shape[1]
    frames = lax.axis_index("tm") * frames_here + jnp.arange(frames_here, dtype=jnp.int32)
    present = (frames[None, :] >= valid_from[:, None])[:, :, None, None, None]
    masked = jnp.where(present, video_clip, jnp.zeros_like(video_clip))
    normed, unit_rows, inverse = norm_forward(masked, norm_gain)
    padded = extended(normed, (("height", 2),), 1)
    pre_activation = spatial(padded, spatial_weight)
    active = jax.nn.silu(pre_activation).astype(jnp.bfloat16)
    prior_frame = shifted(active[:, frames_here - 1 :], "tm", 1)
    even_frames, odd_frames, prior_odd = split_frames(active, prior_frame)
    strided = temporal_forward(even_frames, odd_frames, prior_odd, temporal_weight)
    regrouped = lax.all_to_all(strided, "tm", split_axis=2, concat_axis=1, tiled=True)
    encoded, history = mix_forward(regrouped, mix_weight)
    mix_gradient, regrouped_gradient = mix_backward(history, cotangent, mix_weight)
    strided_gradient = lax.all_to_all(
        regrouped_gradient, "tm", split_axis=1, concat_axis=2, tiled=True
    )
    following = shifted(strided_gradient[:, :1], "tm", -1)
    active_gradient, temporal_gradient = temporal_backward(
        even_frames, odd_frames, prior_odd, strided_gradient, following, temporal_weight
    )
    pre_gradient = activation_backward(active_gradient, pre_activation)
    spatial_gradient = spatial_grad(padded, pre_gradient)
    gradient_padded = extended(pre_gradient, (("height", 2),), 1)
    normed_gradient = spatial(gradient_padded, flipped(spatial_weight))
    video_gradient, gain_gradient = norm_backward(
        normed_gradient, unit_rows, inverse, norm_gain, present
    )
    mix_gradient, temporal_gradient, spatial_gradient, gain_gradient = lax.psum(
        (mix_gradient, temporal_gradient, spatial_gradient, gain_gradient), ("tm", "height", "cam")
    )
    cell_count = (
        video_clip.shape[0]
        * lax.axis_size("cam")
        * frames_here
        * lax.axis_size("tm")
        * video_clip.shape[2]
        * lax.axis_size("height")
        * video_clip.shape[3]
    )
    gradient_scale = 1.0 / math.sqrt(cell_count)
    return (
        encoded,
        video_gradient,
        spatial_gradient * gradient_scale,
        temporal_gradient * gradient_scale,
        mix_gradient * gradient_scale,
        gain_gradient * gradient_scale,
    )


def solution(mesh):
    return jax.shard_map(
        on_device,
        mesh=mesh,
        in_specs=(
            P("cam", "tm", "height", None, None),
            P("cam"),
            P(),
            P(),
            P(),
            P(),
            P("cam", None, ("height", "tm"), None, None),
        ),
        out_specs=(
            P("cam", None, ("height", "tm"), None, None),
            P("cam", "tm", "height", None, None),
            P(),
            P(),
            P(),
            P(),
        ),
        check_vma=False,
    )
```

profile of v0, /device:TPU:2, one launch (start us, length us, event | category | flops | bytes accessed | tf_op | source)
XLA Modules:
  0.0 402.6 jit_solution(15002015680635062406)
XLA Ops:
  12.0 3.5 collective-permute-start
  15.5 4.5 %collective-permute-start.1 = (bf16[1,4,1,64,256]{4,3,2,1,0:T(8,128)(2,1)}, bf16[1,4,1,64,256]{4,3,2,1,0:T(8,128)(2,1)S(1)}, u32[]{:S(2)}, u32[]{:S(2)}) collective-permute-start(bf16[1,4,1,64,256]{4,3,2,1,0:T(8,128)(2,1)} %get-tuple-element.43), channel_id=1, source_target_pairs={{2,0},{4,2},{6,4},{8,6},{10,8},{12,10},{14,12},{16,14},{18,16},{20... | collective-permute-start | bytes 393224 | tf_op jit(solution)/shard_map/ppermute | solution.py:16
  21.8 8.5 %all-to-all-start.1 = ((bf16[1,16,1,64,256]{4,3,2,0,1:T(8,128)(2,1)}), bf16[1,16,1,64,256]{4,3,2,0,1:T(8,128)(2,1)S(1)}, u32[]{:S(2)}, u32[]{:S(2)}) async-start(bf16[1,16,1,64,256]{4,3,2,0,1:T(8,128)(2,1)} %fusion.23), calls=%async_computation.1 | async-start | bytes 1048576 | tf_op jit(solution)/shard_map/all_to_all | solution.py:201
  33.6 2.5 reverse_bitcast_fusion
  40.5 1.8 fusion.46
  42.3 1.9 fusion.51
  44.2 1.8 fusion.47
  53.6 7.1 %collective-permute-done.3 = bf16[1,1,8,64,256]{4,3,2,1,0:T(8,128)(2,1)S(1)} collective-permute-done((bf16[1,1,8,64,256]{4,3,2,1,0:T(8,128)(2,1)S(1)}, bf16[1,1,8,64,256]{4,3,2,1,0:T(8,128)(2,1)S(1)}, u32[]{:S(2)}, u32[]{:S(2)}) %collective-permute-start.3) | collective-permute-done | bytes 262176 | tf_op jit(solution)/shard_map/ppermute | solution.py:24
  64.6 3.2 fusion.14
  71.9 3.8 collective-permute-start.2
  76.0 1.9 collective-permute-start.4
  77.9 6.2 %collective-permute-start.5 = (bf16[1,4,1,64,256]{4,3,2,1,0:T(8,128)(2,1)S(1)}, bf16[1,4,1,64,256]{4,3,2,1,0:T(8,128)(2,1)S(1)}, u32[]{:S(2)}, u32[]{:S(2)}) collective-permute-start(bf16[1,4,1,64,256]{4,3,2,1,0:T(8,128)(2,1)S(1)} %get-tuple-element.41), channel_id=1, source_target_pairs={{2,0},{4,2},{6,4},{8,6},{10,8},{12,10},{14,12},{16,14},{18,16},{20... | collective-permute-start | bytes 393224 | tf_op jit(solution)/shard_map/ppermute | solution.py:16
  95.5 1.8 fusion.31
  100.6 5.8 %all-to-all-start = ((bf16[1,2,8,64,256]{4,3,1,0,2:T(8,128)(2,1)}), bf16[1,2,8,64,256]{4,3,1,0,2:T(8,128)(2,1)}, u32[]{:S(2)}, u32[]{:S(2)}) async-start(bf16[1,2,8,64,256]{4,3,1,0,2:T(8,128)(2,1)} %copy.41), calls=%async_computation | async-start | bytes 1048576 | tf_op jit(solution)/shard_map/all_to_all | solution.py:198
  106.5 2.8 fusion.35
  109.3 2.7 fusion.33
  111.9 2.7 fusion.38
  115.0 6.2 %all-to-all-done = bf16[1,2,8,64,256]{4,3,1,0,2:T(8,128)(2,1)} async-done(((bf16[1,2,8,64,256]{4,3,1,0,2:T(8,128)(2,1)}), bf16[1,2,8,64,256]{4,3,1,0,2:T(8,128)(2,1)}, u32[]{:S(2)}, u32[]{:S(2)}) %all-to-all-start) | async-done | bytes 524320 | tf_op jit(solution)/shard_map/all_to_all | solution.py:198
  127.9 7.8 %fusion.11 = (f32[256]{0:T(256)S(1)}, f32[4,8,64]{2,1,0:T(8,128)S(1)}, f32[4,8,64,256]{3,2,1,0:T(8,128)}) fusion(f32[4,8,64]{2,1,0:T(8,128)S(1)} %add_rsqrt_fusion, bf16[1,4,8,64,256]{4,3,2,1,0:T(8,128)(2,1)S(1)} %copy-done.2, pred[4]{0:T(512)(128)(4,1)S(1)} %add_compare_fusion, f32[256]{0:T(256)S(1)} %copy-done.32, f32[4,8,64,256]{3,2,1,0:T(8,128)} %fusion.26, ...), kind=kOutput, calls=%fused_computation.16 | convolution fusion | flops 277346048 | bytes 21252100 | tf_op jit(solution)/shard_map/dot_general | solution.py:29
  135.7 71.9 %psum.31 = f32[256]{0:T(256)S(1)} all-reduce(f32[256]{0:T(256)S(1)} %get-tuple-element.30), channel_id=1, replica_groups=mesh['tm'=8,'height'=16,'cam'=2] {'tm','height','cam'}, use_global_device_ids=true, to_apply=%region_6.7 | all-reduce | flops 256 | bytes 2048 | tf_op jit(solution)/shard_map/psum | solution.py:215
  208.2 2.9 fusion.10
  213.9 2.1 fusion.24
  216.0 174.5 %all-reduce.7.cloned.1.call-done = (f32[3,3,256,256]{3,2,1,0:T(8,128)}, f32[3,256,256]{2,1,0:T(8,128)}, f32[3,256,256]{2,1,0:T(8,128)}) async-done(((f32[3,3,256,256]{3,2,1,0:T(8,128)}, f32[3,256,256]{2,1,0:T(8,128)}, f32[3,256,256]{2,1,0:T(8,128)}), (f32[3,3,256,256]{3,2,1,0:T(8,128)}, f32[3,256,256]{2,1,0:T(8,128)}, f32[3,256,256]{2,1,0:T(8,128)})) %all-reduce.7.cloned.1.call-update) | async-done | bytes 3932176 | tf_op jit(solution)/shard_map/psum | solution.py:215
  390.5 3.4 broadcast_multiply_fusion
  (136 shorter events, 56.2 us)
Async XLA Ops:
  7.2 12.8 %copy-start.3 = (bf16[1,16,1,64,256]{4,3,2,1,0:T(8,128)(2,1)S(1)}, bf16[1,16,1,64,256]{4,3,2,1,0:T(8,128)(2,1)}, u32[]{:S(2)}) copy-start(bf16[1,16,1,64,256]{4,3,2,1,0:T(8,128)(2,1)} %param.13) | copy-start | bytes 1572868
  7.2 12.8 %copy-start.17 = (bf16[3,256,256]{2,1,0:T(8,128)(2,1)S(1)}, bf16[3,256,256]{2,1,0:T(8,128)(2,1)}, u32[]{:S(2)}) copy-start(bf16[3,256,256]{2,1,0:T(8,128)(2,1)} %param.12) | copy-start | bytes 1179652
  11.2 31.1 %copy-start = (bf16[1,4,8,64,256]{4,3,2,1,0:T(8,128)(2,1)}, bf16[1,4,8,64,256]{4,3,2,1,0:T(8,128)(2,1)S(1)}, u32[]{:S(2)}) copy-start(bf16[1,4,8,64,256]{4,3,2,1,0:T(8,128)(2,1)S(1)} %fusion.5) | copy-start | bytes 3145732
  12.0 24.0 %collective-permute-start = (bf16[1,4,1,64,256]{4,3,2,1,0:T(8,128)(2,1)}, bf16[1,4,1,64,256]{4,3,2,1,0:T(8,128)(2,1)S(1)}, u32[]{:S(2)}, u32[]{:S(2)}) collective-permute-start(bf16[1,4,1,64,256]{4,3,2,1,0:T(8,128)(2,1)} %get-tuple-element.42), channel_id=1, source_target_pairs={{0,2},{2,4},{4,6},{6,8},{8,10},{10,12},{12,14},{14,16},{16,18},{18... | collective-permute-start | bytes 393224 | tf_op jit(solution)/shard_map/ppermute | solution.py:15
  15.5 20.6 %collective-permute-start.1 = (bf16[1,4,1,64,256]{4,3,2,1,0:T(8,128)(2,1)}, bf16[1,4,1,64,256]{4,3,2,1,0:T(8,128)(2,1)S(1)}, u32[]{:S(2)}, u32[]{:S(2)}) collective-permute-start(bf16[1,4,1,64,256]{4,3,2,1,0:T(8,128)(2,1)} %get-tuple-element.43), channel_id=1, source_target_pairs={{2,0},{4,2},{6,4},{8,6},{10,8},{12,10},{14,12},{16,14},{18,16},{20... | collective-permute-start | bytes 393224 | tf_op jit(solution)/shard_map/ppermute | solution.py:16
  20.7 9.6 %copy-start.14 = (bf16[3,3,256,256]{3,2,1,0:T(8,128)(2,1)S(1)}, bf16[3,3,256,256]{3,2,1,0:T(8,128)(2,1)}, u32[]{:S(2)}) copy-start(bf16[3,3,256,256]{3,2,1,0:T(8,128)(2,1)} %param.10) | copy-start | bytes 3538948
  21.8 27.7 %all-to-all-start.1 = ((bf16[1,16,1,64,256]{4,3,2,0,1:T(8,128)(2,1)}), bf16[1,16,1,64,256]{4,3,2,0,1:T(8,128)(2,1)S(1)}, u32[]{:S(2)}, u32[]{:S(2)}) async-start(bf16[1,16,1,64,256]{4,3,2,0,1:T(8,128)(2,1)} %fusion.23), calls=%async_computation.1 | async-start | bytes 1048576 | tf_op jit(solution)/shard_map/all_to_all | solution.py:201
  36.1 6.2 %copy-start.29 = (bf16[1,4,1,64,256]{4,3,2,1,0:T(8,128)(2,1)}, bf16[1,4,1,64,256]{4,3,2,1,0:T(8,128)(2,1)S(1)}, u32[]{:S(2)}) copy-start(bf16[1,4,1,64,256]{4,3,2,1,0:T(8,128)(2,1)S(1)} %collective-permute-done) | copy-start | bytes 393220
  47.7 5.2 %copy-start.19 = (bf16[3,256,256]{2,1,0:T(8,128)(2,1)S(1)}, bf16[3,256,256]{2,1,0:T(8,128)(2,1)}, u32[]{:S(2)}) copy-start(bf16[3,256,256]{2,1,0:T(8,128)(2,1)} %param.11) | copy-start | bytes 1179652
  50.3 11.2 %copy-start.13 = (f32[4,8,64,256]{3,2,1,0:T(8,128)S(1)}, f32[4,8,64,256]{3,2,1,0:T(8,128)}, u32[]{:S(2)}) copy-start(f32[4,8,64,256]{3,2,1,0:T(8,128)} %fusion.49) | copy-start | bytes 6291460
  51.6 9.1 %collective-permute-start.3 = (bf16[1,1,8,64,256]{4,3,2,1,0:T(8,128)(2,1)S(1)}, bf16[1,1,8,64,256]{4,3,2,1,0:T(8,128)(2,1)S(1)}, u32[]{:S(2)}, u32[]{:S(2)}) collective-permute-start(bf16[1,1,8,64,256]{4,3,2,1,0:T(8,128)(2,1)S(1)} %get-tuple-element.47), channel_id=1, source_target_pairs={{32,0},{64,32},{96,64},{128,96},{160,128},{192,160},{224,192},{33,... | collective-permute-start | bytes 786440 | tf_op jit(solution)/shard_map/ppermute | solution.py:24
  52.9 8.7 %copy-start.12 = (f32[4,8,64,256]{3,2,1,0:T(8,128)S(1)}, f32[4,8,64,256]{3,2,1,0:T(8,128)}, u32[]{:S(2)}) copy-start(f32[4,8,64,256]{3,2,1,0:T(8,128)} %fusion.48) | copy-start | bytes 6291460
  53.3 8.3 %copy-start.11 = (f32[4,8,64,256]{3,2,1,0:T(8,128)S(1)}, f32[4,8,64,256]{3,2,1,0:T(8,128)}, u32[]{:S(2)}) copy-start(f32[4,8,64,256]{3,2,1,0:T(8,128)} %fusion.47) | copy-start | bytes 6291460
  61.3 3.3 copy-start.7
  71.3 4.3 %copy-start.20 = (bf16[3,256,256]{2,1,0:T(8,128)(2,1)S(1)}, bf16[3,256,256]{2,1,0:T(8,128)(2,1)}, u32[]{:S(2)}) copy-start(bf16[3,256,256]{2,1,0:T(8,128)(2,1)} %param.11) | copy-start | bytes 1179652
  71.8 12.3 %copy-start.16 = (bf16[3,3,256,256]{3,2,1,0:T(8,128)(2,1)S(1)}, bf16[3,3,256,256]{3,2,1,0:T(8,128)(2,1)}, u32[]{:S(2)}) copy-start(bf16[3,3,256,256]{3,2,1,0:T(8,128)(2,1)} %reverse_bitcast_fusion) | copy-start | bytes 3538948
  71.9 27.2 %collective-permute-start.2 = (bf16[1,1,8,64,256]{4,3,2,1,0:T(8,128)(2,1)S(1)}, bf16[1,1,8,64,256]{4,3,2,1,0:T(8,128)(2,1)S(1)}, u32[]{:S(2)}, u32[]{:S(2)}) collective-permute-start(bf16[1,1,8,64,256]{4,3,2,1,0:T(8,128)(2,1)S(1)} %slice.255), channel_id=1, source_target_pairs={{0,32},{32,64},{64,96},{96,128},{128,160},{160,192},{192,224},{1,3... | collective-permute-start | bytes 786440 | tf_op jit(solution)/shard_map/ppermute | solution.py:24
  76.0 15.1 %collective-permute-start.4 = (bf16[1,4,1,64,256]{4,3,2,1,0:T(8,128)(2,1)S(1)}, bf16[1,4,1,64,256]{4,3,2,1,0:T(8,128)(2,1)S(1)}, u32[]{:S(2)}, u32[]{:S(2)}) collective-permute-start(bf16[1,4,1,64,256]{4,3,2,1,0:T(8,128)(2,1)S(1)} %get-tuple-element.40), channel_id=1, source_target_pairs={{0,2},{2,4},{4,6},{6,8},{8,10},{10,12},{12,14},{14,16},{16,18},{18... | collective-permute-start | bytes 393224 | tf_op jit(solution)/shard_map/ppermute | solution.py:15
  77.9 13.2 %collective-permute-start.5 = (bf16[1,4,1,64,256]{4,3,2,1,0:T(8,128)(2,1)S(1)}, bf16[1,4,1,64,256]{4,3,2,1,0:T(8,128)(2,1)S(1)}, u32[]{:S(2)}, u32[]{:S(2)}) collective-permute-start(bf16[1,4,1,64,256]{4,3,2,1,0:T(8,128)(2,1)S(1)} %get-tuple-element.41), channel_id=1, source_target_pairs={{2,0},{4,2},{6,4},{8,6},{10,8},{12,10},{14,12},{16,14},{18,16},{20... | collective-permute-start | bytes 393224 | tf_op jit(solution)/shard_map/ppermute | solution.py:16
  100.6 20.6 %all-to-all-start = ((bf16[1,2,8,64,256]{4,3,1,0,2:T(8,128)(2,1)}), bf16[1,2,8,64,256]{4,3,1,0,2:T(8,128)(2,1)}, u32[]{:S(2)}, u32[]{:S(2)}) async-start(bf16[1,2,8,64,256]{4,3,1,0,2:T(8,128)(2,1)} %copy.41), calls=%async_computation | async-start | bytes 1048576 | tf_op jit(solution)/shard_map/all_to_all | solution.py:198
  106.4 284.1 %all-reduce.7.cloned.1.call-start = ((), (), s32[]{:S(2)}) async-start(), calls=%async_computation.2 | async-start | bytes 7864320 | tf_op jit(solution)/shard_map/psum | solution.py:215
  114.6 6.6 %copy-start.4 = (bf16[1,16,1,64,256]{4,3,2,1,0:T(8,128)(2,1)S(1)}, bf16[1,16,1,64,256]{4,3,2,1,0:T(8,128)(2,1)}, u32[]{:S(2)}) copy-start(bf16[1,16,1,64,256]{4,3,2,1,0:T(8,128)(2,1)} %param.13) | copy-start | bytes 1572868
  390.5 3.4 copy-start.26
  390.5 4.3 %copy-start.25 = (f32[3,256,256]{2,1,0:T(8,128)S(1)}, f32[3,256,256]{2,1,0:T(8,128)}, u32[]{:S(2)}) copy-start(f32[3,256,256]{2,1,0:T(8,128)} %get-tuple-element.33) | copy-start | bytes 2359300
  (18 other events, 39.3 us)
Sparse Core Ops, SparseCore 0:
  126.8 263.6 all-reduce.6
where the time goes:
time: 404 us; the launch traced here: 403 us
  waiting for transfers between devices  188 us (47%)
  blocking collectives  71.9 us (18%)
  matrix products  62.2 us (15%)
  starting transfers between devices  35.4 us (9%)
  other arithmetic  16.8 us (4%)
  between operations  15.3 us (4%)
  local copies, waits for them, and re-layouts  13.2 us (3%)
    psum x1, waiting for transfers between devices, on_device(): lax.psum((mix_gradient, temporal_gradient, spatial_gradient, gain_gradien...  174 us
    psum x1, blocking collectives, on_device(): lax.psum((mix_gradient, temporal_gradient, spatial_gradient, gain_gradien...  71.9 us
    dot_general x24, matrix products, project(): product = jnp.dot(flat_rows, weight, preferred_element_type=jnp.float32)  48.4 us
    dot_general x15, matrix products, outer_sum(): lax.dot_general(left_rows.reshape(-1, left_rows.shape[-1]), right_rows.re...  10.9 us
    ppermute x2, starting transfers between devices, extended(): after = lax.ppermute(initial, axis, down)  10.7 us
    all_to_all x1, starting transfers between devices, on_device(): lax.all_to_all(regrouped_gradient, 'tm', split_axis=1, concat_axis=2, til...  8.46 us
  transfers between devices with their start and end apart: 9, of which 3 were waited for; matrix products, arithmetic and copies ran while one was open for 15% of the time, Pallas kernels for 0%

commit v1 on v0

--- a/solution.py
+++ b/solution.py
@@ -1,8 +1,18 @@
+import functools
 import math
 import jax
 import jax.numpy as jnp
 from jax import lax
 from jax.sharding import PartitionSpec as P
+
+
+def bind_ends(payload, link_axis, row_axis):
+    for w in (link_axis, row_axis):
+        payload = jax.lax.psum(payload, axis_name=w)
+    return payload
+
+
+masks_map = functools.partial(bind_ends, link_axis="tm", row_axis=("height", "cam"))
 
 
 def extended(array, sides, width):
@@ -212,8 +222,8 @@
     video_gradient, gain_gradient = norm_backward(
         normed_gradient, unit_rows, inverse, norm_gain, present
     )
-    mix_gradient, temporal_gradient, spatial_gradient, gain_gradient = lax.psum(
-        (mix_gradient, temporal_gradient, spatial_gradient, gain_gradient), ("tm", "height", "cam")
+    mix_gradient, temporal_gradient, spatial_gradient, gain_gradient = masks_map(
+        (mix_gradient, temporal_gradient, spatial_gradient, gain_gradient)
     )
     cell_count = (
         video_clip.shape[0]

time: 404 us -> 342 us (0.85)
  waiting for transfers between devices: 188 us -> 127 us
    psum x1 -> x2, waiting for transfers between devices: 174 us -> 112 us  [bind_ends(): payload = jax.lax.psum(payload, axis_name=w)]
    dot_general x24, matrix products: 48.4 us -> 43.9 us  [project(): product = jnp.dot(flat_rows, weight, preferred_element_type=jnp.float32)]
    psum x1 -> x2, blocking collectives: 71.9 us -> 68.8 us  [bind_ends(): payload = jax.lax.psum(payload, axis_name=w)]
  transfers between devices with their start and end apart: 9 -> 10, of which waited for: 3 -> 7; matrix products, arithmetic and copies ran while one was open for 15% -> 18% of each run, Pallas kernels for 0% -> 0%
where the time goes in v1:
time: 342 us; the launch traced here: 340 us
  waiting for transfers between devices  127 us (37%)
  blocking collectives  68.8 us (20%)
  matrix products  58.7 us (17%)
  starting transfers between devices  38.6 us (11%)
  other arithmetic  19.1 us (6%)
  between operations  15.3 us (4%)
  local copies, waits for them, and re-layouts  12.1 us (4%)
    psum x2, waiting for transfers between devices, bind_ends(): payload = jax.lax.psum(payload, axis_name=w)  112 us
    psum x2, blocking collectives, bind_ends(): payload = jax.lax.psum(payload, axis_name=w)  68.8 us
    dot_general x24, matrix products, project(): product = jnp.dot(flat_rows, weight, preferred_element_type=jnp.float32)  43.9 us
    dot_general x15, matrix products, outer_sum(): lax.dot_general(left_rows.reshape(-1, left_rows.shape[-1]), right_rows.re...  12 us
    ppermute x2, starting transfers between devices, extended(): after = lax.ppermute(initial, axis, down)  10.5 us
    all_to_all x1, starting transfers between devices, on_device(): lax.all_to_all(strided, 'tm', split_axis=2, concat_axis=1, tiled=True)  8.9 us
    all_to_all x1, starting transfers between devices, on_device(): lax.all_to_all(regrouped_gradient, 'tm', split_axis=1, concat_axis=2, til...  8.48 us
    unnamed x71, local copies, waits for them, and re-layouts  7.22 us
  transfers between devices with their start and end apart: 10, of which 7 were waited for; matrix products, arithmetic and copies ran while one was open for 18% of the time, Pallas kernels for 0%

profile of v1, /device:TPU:2, one launch (start us, length us, event | category | flops | bytes accessed | tf_op | source)
XLA Modules:
  0.0 340.1 jit_solution(17189298792950957436)
XLA Ops:
  11.3 3.5 %collective-permute-start = (bf16[1,4,1,64,256]{4,3,2,1,0:T(8,128)(2,1)S(1)}, bf16[1,4,1,64,256]{4,3,2,1,0:T(8,128)(2,1)S(1)}, u32[]{:S(2)}, u32[]{:S(2)}) collective-permute-start(bf16[1,4,1,64,256]{4,3,2,1,0:T(8,128)(2,1)S(1)} %get-tuple-element.45), channel_id=1, source_target_pairs={{0,2},{2,4},{4,6},{6,8},{8,10},{10,12},{12,14},{14,16},{16,18},{18... | collective-permute-start | bytes 393224 | tf_op jit(solution)/shard_map/ppermute | solution.py:25
  14.8 4.5 %collective-permute-start.1 = (bf16[1,4,1,64,256]{4,3,2,1,0:T(8,128)(2,1)S(1)}, bf16[1,4,1,64,256]{4,3,2,1,0:T(8,128)(2,1)S(1)}, u32[]{:S(2)}, u32[]{:S(2)}) collective-permute-start(bf16[1,4,1,64,256]{4,3,2,1,0:T(8,128)(2,1)S(1)} %get-tuple-element.46), channel_id=1, source_target_pairs={{2,0},{4,2},{6,4},{8,6},{10,8},{12,10},{14,12},{16,14},{18,16},{20... | collective-permute-start | bytes 393224 | tf_op jit(solution)/shard_map/ppermute | solution.py:26
  21.1 8.5 %all-to-all-start.1 = ((bf16[1,16,1,64,256]{4,3,2,0,1:T(8,128)(2,1)}), bf16[1,16,1,64,256]{4,3,2,0,1:T(8,128)(2,1)S(1)}, u32[]{:S(2)}, u32[]{:S(2)}) async-start(bf16[1,16,1,64,256]{4,3,2,0,1:T(8,128)(2,1)} %fusion.23), calls=%async_computation.1 | async-start | bytes 1048576 | tf_op jit(solution)/shard_map/all_to_all | solution.py:211
  29.6 2.7 fusion.42
  39.0 1.8 fusion.51
  40.9 1.8 fusion.47
  50.6 6.9 %collective-permute-done.3 = bf16[1,1,8,64,256]{4,3,2,1,0:T(8,128)(2,1)S(1)} collective-permute-done((bf16[1,1,8,64,256]{4,3,2,1,0:T(8,128)(2,1)S(1)}, bf16[1,1,8,64,256]{4,3,2,1,0:T(8,128)(2,1)S(1)}, u32[]{:S(2)}, u32[]{:S(2)}) %collective-permute-start.3) | collective-permute-done | bytes 262176 | tf_op jit(solution)/shard_map/ppermute | solution.py:34
  61.3 3.2 fusion.14
  70.8 4.0 %collective-permute-start.2 = (bf16[1,1,8,64,256]{4,3,2,1,0:T(8,128)(2,1)S(1)}, bf16[1,1,8,64,256]{4,3,2,1,0:T(8,128)(2,1)S(1)}, u32[]{:S(2)}, u32[]{:S(2)}) collective-permute-start(bf16[1,1,8,64,256]{4,3,2,1,0:T(8,128)(2,1)S(1)} %slice.255), channel_id=1, source_target_pairs={{0,32},{32,64},{64,96},{96,128},{128,160},{160,192},{192,224},{1,3... | collective-permute-start | bytes 786440 | tf_op jit(solution)/shard_map/ppermute | solution.py:34
  80.6 8.9 %all-to-all-start = ((bf16[1,2,8,64,256]{4,3,1,0,2:T(8,128)(2,1)}), bf16[1,2,8,64,256]{4,3,1,0,2:T(8,128)(2,1)S(1)}, u32[]{:S(2)}, u32[]{:S(2)}) async-start(bf16[1,2,8,64,256]{4,3,1,0,2:T(8,128)(2,1)} %copy.41), calls=%async_computation | async-start | bytes 1048576 | tf_op jit(solution)/shard_map/all_to_all | solution.py:208
  90.8 2.1 convolution_bitcast_fusion.8
  92.9 2.1 convolution_bitcast_fusion.9
  96.9 6.9 %all-to-all-done = bf16[1,2,8,64,256]{4,3,1,0,2:T(8,128)(2,1)S(1)} async-done(((bf16[1,2,8,64,256]{4,3,1,0,2:T(8,128)(2,1)}), bf16[1,2,8,64,256]{4,3,1,0,2:T(8,128)(2,1)S(1)}, u32[]{:S(2)}, u32[]{:S(2)}) %all-to-all-start) | async-done | bytes 524320 | tf_op jit(solution)/shard_map/all_to_all | solution.py:208
  106.5 2.4 copy.47
  110.3 1.9 collective-permute-start.4
  112.3 6.0 %collective-permute-start.5 = (bf16[1,4,1,64,256]{4,3,2,1,0:T(8,128)(2,1)S(1)}, bf16[1,4,1,64,256]{4,3,2,1,0:T(8,128)(2,1)S(1)}, u32[]{:S(2)}, u32[]{:S(2)}) collective-permute-start(bf16[1,4,1,64,256]{4,3,2,1,0:T(8,128)(2,1)S(1)} %get-tuple-element.44), channel_id=1, source_target_pairs={{2,0},{4,2},{6,4},{8,6},{10,8},{12,10},{14,12},{16,14},{18,16},{20... | collective-permute-start | bytes 393224 | tf_op jit(solution)/shard_map/ppermute | solution.py:26
  118.3 1.9 fusion.77
  134.0 71.2 %all-reduce.11.cloned.1.call-done = (f32[3,3,256,256]{3,2,1,0:T(8,128)}, f32[3,256,256]{2,1,0:T(8,128)}, f32[3,256,256]{2,1,0:T(8,128)}) async-done(((f32[3,3,256,256]{3,2,1,0:T(8,128)}, f32[3,256,256]{2,1,0:T(8,128)}, f32[3,256,256]{2,1,0:T(8,128)}), (f32[3,3,256,256]{3,2,1,0:T(8,128)}, f32[3,256,256]{2,1,0:T(8,128)}, f32[3,256,256]{2,1,0:T(8,128)})) %all-reduce.11.cloned.1.call-update) | async-done | bytes 3932176 | tf_op jit(solution)/shard_map/psum | solution.py:11
  205.3 7.6 %fusion.11 = (f32[256]{0:T(256)S(1)}, f32[4,8,64]{2,1,0:T(8,128)S(1)}, f32[4,8,64,256]{3,2,1,0:T(8,128)}) fusion(f32[4,8,64]{2,1,0:T(8,128)S(1)} %add_rsqrt_fusion, bf16[1,4,8,64,256]{4,3,2,1,0:T(8,128)(2,1)S(1)} %copy-done.2, pred[4]{0:T(512)(128)(4,1)S(1)} %copy-done.34, f32[256]{0:T(256)S(1)} %copy-done.32, f32[4,8,64,256]{3,2,1,0:T(8,128)} %fusion.26, ...), kind=kOutput, calls=%fused_computation.16 | convolution fusion | flops 277346048 | bytes 21252100 | tf_op jit(solution)/shard_map/dot_general | solution.py:39
  212.8 15.5 %psum.62 = f32[256]{0:T(256)S(1)} all-reduce(f32[256]{0:T(256)S(1)} %get-tuple-element.30), channel_id=1, replica_groups=mesh['tm'=8,'height'=16,'cam'=2] {'tm'}, use_global_device_ids=true, to_apply=%region_9.10 | all-reduce | flops 256 | bytes 2048 | tf_op jit(solution)/shard_map/psum | solution.py:11
  228.3 53.3 %psum.63 = f32[256]{0:T(256)S(1)} all-reduce(f32[256]{0:T(256)S(1)} %psum.62), channel_id=1, replica_groups=mesh['tm'=8,'height'=16,'cam'=2] {'height','cam'}, use_global_device_ids=true, to_apply=%region_10.11 | all-reduce | flops 256 | bytes 2048 | tf_op jit(solution)/shard_map/psum | solution.py:11
  282.2 2.9 fusion.10
  286.8 41.1 %all-reduce.9.cloned.1.call-done = (f32[3,3,256,256]{3,2,1,0:T(8,128)}, f32[3,256,256]{2,1,0:T(8,128)}, f32[3,256,256]{2,1,0:T(8,128)}) async-done(((f32[3,3,256,256]{3,2,1,0:T(8,128)}, f32[3,256,256]{2,1,0:T(8,128)}, f32[3,256,256]{2,1,0:T(8,128)}), (f32[3,3,256,256]{3,2,1,0:T(8,128)}, f32[3,256,256]{2,1,0:T(8,128)}, f32[3,256,256]{2,1,0:T(8,128)})) %all-reduce.9.cloned.1.call-update) | async-done | bytes 3932176 | tf_op jit(solution)/shard_map/psum | solution.py:11
  327.9 3.4 broadcast_multiply_fusion
  (144 shorter events, 60.7 us)
Async XLA Ops:
  7.2 12.1 %copy-start.3 = (bf16[1,16,1,64,256]{4,3,2,1,0:T(8,128)(2,1)S(1)}, bf16[1,16,1,64,256]{4,3,2,1,0:T(8,128)(2,1)}, u32[]{:S(2)}) copy-start(bf16[1,16,1,64,256]{4,3,2,1,0:T(8,128)(2,1)} %param.13) | copy-start | bytes 1572868
  7.2 12.1 %copy-start.18 = (bf16[3,256,256]{2,1,0:T(8,128)(2,1)S(1)}, bf16[3,256,256]{2,1,0:T(8,128)(2,1)}, u32[]{:S(2)}) copy-start(bf16[3,256,256]{2,1,0:T(8,128)(2,1)} %param.12) | copy-start | bytes 1179652
  11.3 27.8 %copy-start = (bf16[1,4,8,64,256]{4,3,2,1,0:T(8,128)(2,1)}, bf16[1,4,8,64,256]{4,3,2,1,0:T(8,128)(2,1)S(1)}, u32[]{:S(2)}) copy-start(bf16[1,4,8,64,256]{4,3,2,1,0:T(8,128)(2,1)S(1)} %fusion.5) | copy-start | bytes 3145732
  11.3 21.0 %collective-permute-start = (bf16[1,4,1,64,256]{4,3,2,1,0:T(8,128)(2,1)S(1)}, bf16[1,4,1,64,256]{4,3,2,1,0:T(8,128)(2,1)S(1)}, u32[]{:S(2)}, u32[]{:S(2)}) collective-permute-start(bf16[1,4,1,64,256]{4,3,2,1,0:T(8,128)(2,1)S(1)} %get-tuple-element.45), channel_id=1, source_target_pairs={{0,2},{2,4},{4,6},{6,8},{8,10},{10,12},{12,14},{14,16},{16,18},{18... | collective-permute-start | bytes 393224 | tf_op jit(solution)/shard_map/ppermute | solution.py:25
  14.8 17.5 %collective-permute-start.1 = (bf16[1,4,1,64,256]{4,3,2,1,0:T(8,128)(2,1)S(1)}, bf16[1,4,1,64,256]{4,3,2,1,0:T(8,128)(2,1)S(1)}, u32[]{:S(2)}, u32[]{:S(2)}) collective-permute-start(bf16[1,4,1,64,256]{4,3,2,1,0:T(8,128)(2,1)S(1)} %get-tuple-element.46), channel_id=1, source_target_pairs={{2,0},{4,2},{6,4},{8,6},{10,8},{12,10},{14,12},{16,14},{18,16},{20... | collective-permute-start | bytes 393224 | tf_op jit(solution)/shard_map/ppermute | solution.py:26
  21.1 25.4 %all-to-all-start.1 = ((bf16[1,16,1,64,256]{4,3,2,0,1:T(8,128)(2,1)}), bf16[1,16,1,64,256]{4,3,2,0,1:T(8,128)(2,1)S(1)}, u32[]{:S(2)}, u32[]{:S(2)}) async-start(bf16[1,16,1,64,256]{4,3,2,0,1:T(8,128)(2,1)} %fusion.23), calls=%async_computation.1 | async-start | bytes 1048576 | tf_op jit(solution)/shard_map/all_to_all | solution.py:211
  32.3 6.7 %copy-start.29 = (bf16[1,4,1,64,256]{4,3,2,1,0:T(8,128)(2,1)}, bf16[1,4,1,64,256]{4,3,2,1,0:T(8,128)(2,1)S(1)}, u32[]{:S(2)}) copy-start(bf16[1,4,1,64,256]{4,3,2,1,0:T(8,128)(2,1)S(1)} %collective-permute-done) | copy-start | bytes 393220
  44.5 5.4 %copy-start.20 = (bf16[3,256,256]{2,1,0:T(8,128)(2,1)S(1)}, bf16[3,256,256]{2,1,0:T(8,128)(2,1)}, u32[]{:S(2)}) copy-start(bf16[3,256,256]{2,1,0:T(8,128)(2,1)} %param.11) | copy-start | bytes 1179652
  47.3 11.0 %copy-start.13 = (f32[4,8,64,256]{3,2,1,0:T(8,128)S(1)}, f32[4,8,64,256]{3,2,1,0:T(8,128)}, u32[]{:S(2)}) copy-start(f32[4,8,64,256]{3,2,1,0:T(8,128)} %fusion.49) | copy-start | bytes 6291460
  48.6 8.8 %collective-permute-start.3 = (bf16[1,1,8,64,256]{4,3,2,1,0:T(8,128)(2,1)S(1)}, bf16[1,1,8,64,256]{4,3,2,1,0:T(8,128)(2,1)S(1)}, u32[]{:S(2)}, u32[]{:S(2)}) collective-permute-start(bf16[1,1,8,64,256]{4,3,2,1,0:T(8,128)(2,1)S(1)} %get-tuple-element.50), channel_id=1, source_target_pairs={{32,0},{64,32},{96,64},{128,96},{160,128},{192,160},{224,192},{33,... | collective-permute-start | bytes 786440 | tf_op jit(solution)/shard_map/ppermute | solution.py:34
  49.9 8.4 %copy-start.12 = (f32[4,8,64,256]{3,2,1,0:T(8,128)S(1)}, f32[4,8,64,256]{3,2,1,0:T(8,128)}, u32[]{:S(2)}) copy-start(f32[4,8,64,256]{3,2,1,0:T(8,128)} %fusion.48) | copy-start | bytes 6291460
  50.2 8.1 %copy-start.11 = (f32[4,8,64,256]{3,2,1,0:T(8,128)S(1)}, f32[4,8,64,256]{3,2,1,0:T(8,128)}, u32[]{:S(2)}) copy-start(f32[4,8,64,256]{3,2,1,0:T(8,128)} %fusion.47) | copy-start | bytes 6291460
  70.8 7.7 %collective-permute-start.2 = (bf16[1,1,8,64,256]{4,3,2,1,0:T(8,128)(2,1)S(1)}, bf16[1,1,8,64,256]{4,3,2,1,0:T(8,128)(2,1)S(1)}, u32[]{:S(2)}, u32[]{:S(2)}) collective-permute-start(bf16[1,1,8,64,256]{4,3,2,1,0:T(8,128)(2,1)S(1)} %slice.255), channel_id=1, source_target_pairs={{0,32},{32,64},{64,96},{96,128},{128,160},{160,192},{192,224},{1,3... | collective-permute-start | bytes 786440 | tf_op jit(solution)/shard_map/ppermute | solution.py:34
  79.8 9.8 %copy-start.31 = (f32[1,256,256]{2,1,0:T(8,128)S(1)}, f32[1,256,256]{2,1,0:T(8,128)}, u32[]{:S(2)}) copy-start(f32[1,256,256]{2,1,0:T(8,128)} %convolution_bitcast_fusion.11) | copy-start | bytes 786436
  80.6 23.2 %all-to-all-start = ((bf16[1,2,8,64,256]{4,3,1,0,2:T(8,128)(2,1)}), bf16[1,2,8,64,256]{4,3,1,0,2:T(8,128)(2,1)S(1)}, u32[]{:S(2)}, u32[]{:S(2)}) async-start(bf16[1,2,8,64,256]{4,3,1,0,2:T(8,128)(2,1)} %copy.41), calls=%async_computation | async-start | bytes 1048576 | tf_op jit(solution)/shard_map/all_to_all | solution.py:208
  89.5 115.7 %all-reduce.11.cloned.1.call-start = ((), (), s32[]{:S(2)}) async-start(), calls=%async_computation.3 | async-start | bytes 7864320 | tf_op jit(solution)/shard_map/psum | solution.py:11
  96.6 7.3 %copy-start.4 = (bf16[1,16,1,64,256]{4,3,2,1,0:T(8,128)(2,1)S(1)}, bf16[1,16,1,64,256]{4,3,2,1,0:T(8,128)(2,1)}, u32[]{:S(2)}) copy-start(bf16[1,16,1,64,256]{4,3,2,1,0:T(8,128)(2,1)} %param.13) | copy-start | bytes 1572868
  106.5 221.4 %all-reduce.9.cloned.1.call-start = ((), (), s32[]{:S(2)}) async-start(), calls=%async_computation.2 | async-start | bytes 7864320 | tf_op jit(solution)/shard_map/psum | solution.py:11
  110.3 22.0 %copy-start.15 = (bf16[3,3,256,256]{3,2,1,0:T(8,128)(2,1)}, bf16[3,3,256,256]{3,2,1,0:T(8,128)(2,1)S(1)}, u32[]{:S(2)}) copy-start(bf16[3,3,256,256]{3,2,1,0:T(8,128)(2,1)S(1)} %reverse_bitcast_fusion) | copy-start | bytes 3538948
  110.3 9.8 %collective-permute-start.4 = (bf16[1,4,1,64,256]{4,3,2,1,0:T(8,128)(2,1)S(1)}, bf16[1,4,1,64,256]{4,3,2,1,0:T(8,128)(2,1)S(1)}, u32[]{:S(2)}, u32[]{:S(2)}) collective-permute-start(bf16[1,4,1,64,256]{4,3,2,1,0:T(8,128)(2,1)S(1)} %get-tuple-element.43), channel_id=1, source_target_pairs={{0,2},{2,4},{4,6},{6,8},{8,10},{10,12},{12,14},{14,16},{16,18},{18... | collective-permute-start | bytes 393224 | tf_op jit(solution)/shard_map/ppermute | solution.py:25
  112.3 8.5 %collective-permute-start.5 = (bf16[1,4,1,64,256]{4,3,2,1,0:T(8,128)(2,1)S(1)}, bf16[1,4,1,64,256]{4,3,2,1,0:T(8,128)(2,1)S(1)}, u32[]{:S(2)}, u32[]{:S(2)}) collective-permute-start(bf16[1,4,1,64,256]{4,3,2,1,0:T(8,128)(2,1)S(1)} %get-tuple-element.44), channel_id=1, source_target_pairs={{2,0},{4,2},{6,4},{8,6},{10,8},{12,10},{14,12},{16,14},{18,16},{20... | collective-permute-start | bytes 393224 | tf_op jit(solution)/shard_map/ppermute | solution.py:26
  134.0 71.3 %copy-start.2 = (bf16[1,4,8,64,256]{4,3,2,1,0:T(8,128)(2,1)S(1)}, bf16[1,4,8,64,256]{4,3,2,1,0:T(8,128)(2,1)}, u32[]{:S(2)}) copy-start(bf16[1,4,8,64,256]{4,3,2,1,0:T(8,128)(2,1)} %param.7) | copy-start | bytes 3145732
  134.0 71.3 %copy-start.32 = (f32[256]{0:T(256)S(1)}, f32[256]{0:T(256)}, u32[]{:S(2)}) copy-start(f32[256]{0:T(256)} %param.9) | copy-start | bytes 3076
  134.0 71.3 %copy-start.34 = (pred[4]{0:T(512)(128)(4,1)S(1)}, pred[4]{0:T(512)(128)(4,1)}, u32[]{:S(2)}) copy-start(pred[4]{0:T(512)(128)(4,1)} %copy-done.33) | copy-start | bytes 16
  (21 other events, 55.6 us)
Sparse Core Ops, SparseCore 0:
  106.6 98.5 all-reduce.10
  208.9 118.9 all-reduce.8
